TPU v7x, 32 devices: a whole 2x2x4 slice. The times are simulated.
32 devices in a mesh: dp: 8 (over y, x, core), mp: 4 (over z).
Axes of the slice: x: 2, y: 2, z: 4, core: 2. Of those that a mesh axis runs over, the one named last changes fastest.
Arguments:
- token_ids: int32 [8, 128], P('dp'), may hold values from 0 to 250111
- target_ids: int32 [8, 128], P('dp'), may hold values from 0 to 250111
- segment_ids: int32 [8, 128], P('dp'), may hold values from 0 to 3, never falling along the last dimension, each value on 1 to 64 neighbouring positions
- target_length: int32 [8], P('dp'), may hold values from 64 to 128
- memory_length: int32 [8], P('dp'), may hold values from 64 to 256
- memory: bfloat16 [8, 256, 768], P('dp'), may hold values from -6 to 6
- embed_table: bfloat16 [250112, 768], P(('dp', 'mp')), may hold values from -6 to 6
- head_table: bfloat16 [250112, 768], P(('dp', 'mp')), may hold values from -0.4375 to 0.4375
- self_gain: float32 [768], replicated, may hold values from 0.5 to 1.5
- self_query: bfloat16 [768, 768], P(None, 'mp'), may hold values from -0.109375 to 0.109375
- self_kv: bfloat16 [768, 2, 768], P(None, None, 'mp'), may hold values from -0.109375 to 0.109375
- self_out: bfloat16 [768, 768], P(None, 'mp'), may hold values from -1.5 to 1.5
- cross_gain: float32 [768], replicated, may hold values from 0.5 to 1.5
- cross_query: bfloat16 [768, 768], P(None, 'mp'), may hold values from -0.109375 to 0.109375
- cross_kv: bfloat16 [768, 2, 768], P(None, None, 'mp'), may hold values from -0.109375 to 0.109375
- cross_out: bfloat16 [768, 768], P(None, 'mp'), may hold values from -2 to 2
- ffn_gain: float32 [768], replicated, may hold values from 0.5 to 1.5
- ffn_in: bfloat16 [768, 2, 2048], P(None, None, 'mp'), may hold values from -0.21875 to 0.21875
- ffn_out: bfloat16 [768, 2048], P(None, 'mp'), may hold values from -0.1875 to 0.1875
- final_gain: float32 [768], replicated, may hold values from 0.5 to 1.5
Outputs:
- loss: float32 [], replicated
- memory_grad: float32 [8, 256, 768], P('dp')
- embed_grad: float32 [250112, 768], P(('dp', 'mp'))
- head_grad: float32 [250112, 768], P(('dp', 'mp'))
- self_gain_grad: float32 [768], P('dp')
- self_query_grad: float32 [768, 768], P('dp', 'mp')
- self_kv_grad: float32 [768, 2, 768], P('dp', None, 'mp')
- self_out_grad: float32 [768, 768], P('dp', 'mp')
- cross_gain_grad: float32 [768], P('dp')
- cross_query_grad: float32 [768, 768], P('dp', 'mp')
- cross_kv_grad: float32 [768, 2, 768], P('dp', None, 'mp')
- cross_out_grad: float32 [768, 768], P('dp', 'mp')
- ffn_gain_grad: float32 [768], P('dp')
- ffn_in_grad: float32 [768, 2, 2048], P('dp', None, 'mp')
- ffn_out_grad: float32 [768, 2048], P('dp', 'mp')
- final_gain_grad: float32 [768], P('dp')
Inputs may be any that keep to these rules, and one draw needn't show every extreme that they name: `segment_ids`: within a row the numbers never fall.
All inputs are finite; a program needn't handle non-finite values.
Results may differ from a plain program's by a relative error of at most 0.025.
The roundings to bfloat16 on the way count: a program that leaves them out, or rounds other values in their place, can miss the bound.
Values may be sent and summed in bfloat16 or wider, within the bound.
No kernel may reach another device: no remote copies, remote signals or barrier semaphores. Data moves between devices by JAX's collectives and lax.ppermute only.
A program may use at most 320 MiB of HBM per device.

v0:
```python
import jax
import jax.numpy as jnp
from jax import lax
from jax.sharding import PartitionSpec as P

DH = 64


EPSILON = 1e-06
NEGATIVE = -1e30
CONTRACT_FIRST = (((0,), (0,)), ((), ()))
CONTRACT_LAST = (((1,), (1,)), ((), ()))


def normed(values, gain):
    scale_rows = lax.rsqrt(jnp.mean(values * values, axis=-1, keepdims=True) + EPSILON)
    return values * scale_rows * gain


def norm_back(values, gain, upstream):
    scale_rows = lax.rsqrt(jnp.mean(values * values, axis=-1, keepdims=True) + EPSILON)
    weighted = upstream * gain
    inner_mean = jnp.mean(values * weighted, axis=-1, keepdims=True)
    grad_values = scale_rows * weighted - values * scale_rows * scale_rows * scale_rows * inner_mean
    return (grad_values, jnp.sum(upstream * values * scale_rows, axis=0))


def gelu_tanh(values):
    return jax.nn.gelu(values, approximate=True)


def model_sum(values):
    return lax.psum(values, "mp")


def gather_rows(values):
    return lax.all_gather(values.astype(jnp.bfloat16), "mp", axis=0, tiled=True).astype(
        values.dtype
    )


def attend(queries, key_rows, value_rows, allowed):
    scores = jnp.einsum("qhe,khe->hqk", queries, key_rows, preferred_element_type=jnp.float32)
    scores = jnp.where(allowed, scores, NEGATIVE)
    top_score = jnp.max(scores, axis=-1, keepdims=True)
    log_total = top_score + jnp.log(jnp.sum(jnp.exp(scores - top_score), axis=-1, keepdims=True))
    weights = jnp.exp(scores - log_total).astype(jnp.bfloat16)
    mixed = jnp.einsum("hqk,khe->qhe", weights, value_rows, preferred_element_type=jnp.float32)
    return (mixed.astype(jnp.bfloat16), log_total)


def attend_back(queries, key_rows, value_rows, allowed, log_total, upstream):
    scores = jnp.einsum("qhe,khe->hqk", queries, key_rows, preferred_element_type=jnp.float32)
    scores = jnp.where(allowed, scores, NEGATIVE)
    probs = jnp.exp(scores - log_total)
    weights = probs.astype(jnp.bfloat16)
    pulled = jnp.einsum("qhe,khe->hqk", upstream, value_rows, preferred_element_type=jnp.float32)
    grad_scores = (probs * (pulled - jnp.sum(probs * pulled, axis=-1, keepdims=True))).astype(
        jnp.bfloat16
    )
    grad_queries = jnp.einsum(
        "hqk,khe->qhe", grad_scores, key_rows, preferred_element_type=jnp.float32
    ).astype(jnp.bfloat16)
    grad_keys = jnp.einsum(
        "hqk,qhe->khe", grad_scores, queries, preferred_element_type=jnp.float32
    ).astype(jnp.bfloat16)
    grad_values = jnp.einsum(
        "hqk,qhe->khe", weights, upstream, preferred_element_type=jnp.float32
    ).astype(jnp.bfloat16)
    return (grad_queries, grad_keys, grad_values)


def on_device(
    token_ids,
    target_ids,
    segment_ids,
    target_length,
    memory_length,
    memory,
    embed_table,
    head_table,
    self_gain,
    self_query,
    self_kv,
    self_out,
    cross_gain,
    cross_query,
    cross_kv,
    cross_out,
    ffn_gain,
    ffn_in,
    ffn_out,
    final_gain,
):
    groups = lax.axis_size("dp")
    shards = lax.axis_size("mp")
    group_index = lax.axis_index("dp")
    shard_index = lax.axis_index("mp")
    length = token_ids.shape[1]
    part_rows = length // shards
    own_rows = embed_table.shape[0]
    block_rows = own_rows * shards
    memory_rows = memory.shape[1]
    heads_here = self_query.shape[1] // DH
    positions = jnp.arange(length)
    first_row = shard_index * part_rows
    marked = jnp.where(positions < target_length[0], target_ids[0], -1)
    ids_every, marked_every = (
        lax.all_gather(
            lax.dynamic_slice_in_dim(token_ids[0], first_row, part_rows),
            ("dp", "mp"),
            axis=0,
            tiled=True,
        ),
        lax.all_gather(
            lax.dynamic_slice_in_dim(marked, first_row, part_rows), ("dp", "mp"), axis=0, tiled=True
        ),
    )
    ids_slice = lax.dynamic_index_in_dim(
        ids_every.reshape(groups, shards, part_rows), shard_index, 1, keepdims=False
    ).reshape(-1)
    marked_slice = lax.dynamic_index_in_dim(
        marked_every.reshape(groups, shards, part_rows), shard_index, 1, keepdims=False
    ).reshape(-1)
    embed_block, head_block = (
        lax.all_gather(embed_table, "mp", axis=0, tiled=True),
        lax.all_gather(head_table, "mp", axis=0, tiled=True),
    )
    block_start = group_index * block_rows
    local_ids = ids_slice - block_start
    inside = (local_ids >= 0) & (local_ids < block_rows)
    looked = jnp.take(embed_block, jnp.clip(local_ids, 0, block_rows - 1), axis=0)
    own_part = lax.psum_scatter(
        jnp.where(inside[:, None], looked.astype(jnp.float32), 0.0),
        "dp",
        scatter_dimension=0,
        tiled=True,
    )
    states = gather_rows(own_part)
    normed_self = normed(states, self_gain).astype(jnp.bfloat16)
    queries = (
        jnp.dot(normed_self, self_query, preferred_element_type=jnp.float32)
        .astype(jnp.bfloat16)
        .reshape(length, heads_here, DH)
    )
    key_value = (
        jnp.einsum("td,dch->cth", normed_self, self_kv, preferred_element_type=jnp.float32)
        .astype(jnp.bfloat16)
        .reshape(2, length, heads_here, DH)
    )
    allowed = (positions[:, None] >= positions[None, :]) & (
        segment_ids[0][:, None] == segment_ids[0][None, :]
    )
    self_mix, self_total = attend(queries, key_value[0], key_value[1], allowed)
    self_mix = self_mix.reshape(length, -1)
    after_self = states + model_sum(
        lax.dot_general(self_mix, self_out, CONTRACT_LAST, preferred_element_type=jnp.float32)
    )
    encoder = memory[0]
    normed_cross = normed(after_self, cross_gain).astype(jnp.bfloat16)
    cross_queries = (
        jnp.dot(normed_cross, cross_query, preferred_element_type=jnp.float32)
        .astype(jnp.bfloat16)
        .reshape(length, heads_here, DH)
    )
    cross_pair = (
        jnp.einsum("md,dch->cmh", encoder, cross_kv, preferred_element_type=jnp.float32)
        .astype(jnp.bfloat16)
        .reshape(2, memory_rows, heads_here, DH)
    )
    reachable = (jnp.arange(memory_rows) < memory_length[0])[None, :]
    cross_mix, cross_total = attend(cross_queries, cross_pair[0], cross_pair[1], reachable)
    cross_mix = cross_mix.reshape(length, -1)
    after_cross = after_self + model_sum(
        lax.dot_general(cross_mix, cross_out, CONTRACT_LAST, preferred_element_type=jnp.float32)
    )
    normed_ffn = normed(after_cross, ffn_gain).astype(jnp.bfloat16)
    inner_pre = jnp.einsum("td,dcf->ctf", normed_ffn, ffn_in, preferred_element_type=jnp.float32)
    up_pre = inner_pre[1]
    activated, gelu_pull = jax.vjp(gelu_tanh, inner_pre[0])
    hidden = (activated * up_pre).astype(jnp.bfloat16)
    after_ffn = after_cross + model_sum(
        lax.dot_general(hidden, ffn_out, CONTRACT_LAST, preferred_element_type=jnp.float32)
    )
    final_states = normed(after_ffn, final_gain).astype(jnp.bfloat16)
    final_every = lax.all_gather(
        lax.dynamic_slice_in_dim(final_states, first_row, part_rows), "dp", axis=0, tiled=True
    )
    logits = lax.dot_general(
        final_every, head_block, CONTRACT_LAST, preferred_element_type=jnp.float32
    )
    target_hit = jnp.arange(block_rows)[None, :] == (marked_slice - block_start)[:, None]
    chosen = jnp.sum(jnp.where(target_hit, logits, 0.0), axis=1)
    peak_logit = lax.pmax(jnp.max(logits, axis=1), "dp")
    spread, picked = lax.psum(
        (jnp.sum(jnp.exp(logits - peak_logit[:, None]), axis=1), chosen), "dp"
    )
    log_total = peak_logit + jnp.log(spread)
    keep_mask = (marked_slice >= 0).astype(jnp.float32)
    loss_scale = 1.0 / (groups * length)
    loss_value = model_sum(jnp.sum(keep_mask * (log_total - picked)) * loss_scale)
    probs = jnp.exp(logits - log_total[:, None])
    grad_logits = (
        (probs - target_hit.astype(jnp.float32)) * (keep_mask * loss_scale)[:, None]
    ).astype(jnp.bfloat16)
    grad_final = gather_rows(
        lax.psum_scatter(
            jnp.dot(grad_logits, head_block, preferred_element_type=jnp.float32),
            "dp",
            scatter_dimension=0,
            tiled=True,
        )
    )
    head_grad = lax.psum_scatter(
        lax.dot_general(
            grad_logits, final_every, CONTRACT_FIRST, preferred_element_type=jnp.float32
        ).astype(jnp.bfloat16),
        "mp",
        scatter_dimension=0,
        tiled=True,
    ).astype(jnp.float32)
    grad_after_ffn, final_gain_grad = norm_back(after_ffn, final_gain, grad_final)
    grad_down = grad_after_ffn.astype(jnp.bfloat16)
    ffn_out_grad = lax.dot_general(
        grad_down, hidden, CONTRACT_FIRST, preferred_element_type=jnp.float32
    )
    grad_hidden = jnp.dot(grad_down, ffn_out, preferred_element_type=jnp.float32)
    grad_gate = gelu_pull(grad_hidden * up_pre)[0]
    grad_inner = jnp.stack([grad_gate, grad_hidden * activated]).astype(jnp.bfloat16)
    ffn_in_grad = jnp.einsum(
        "td,ctf->dcf", normed_ffn, grad_inner, preferred_element_type=jnp.float32
    )
    grad_normed_ffn = model_sum(
        jnp.einsum("ctf,dcf->td", grad_inner, ffn_in, preferred_element_type=jnp.float32)
    )
    grad_from_ffn, ffn_gain_grad = norm_back(after_cross, ffn_gain, grad_normed_ffn)
    grad_after_cross = grad_after_ffn + grad_from_ffn
    grad_cross_out = grad_after_cross.astype(jnp.bfloat16)
    cross_out_grad = lax.dot_general(
        grad_cross_out, cross_mix, CONTRACT_FIRST, preferred_element_type=jnp.float32
    )
    grad_cross_mix = (
        jnp.dot(grad_cross_out, cross_out, preferred_element_type=jnp.float32)
        .astype(jnp.bfloat16)
        .reshape(length, heads_here, DH)
    )
    grad_cross_queries, grad_cross_keys, grad_cross_values = attend_back(
        cross_queries, cross_pair[0], cross_pair[1], reachable, cross_total, grad_cross_mix
    )
    grad_cross_queries = grad_cross_queries.reshape(length, -1)
    grad_cross_pair = jnp.stack(
        [grad_cross_keys.reshape(memory_rows, -1), grad_cross_values.reshape(memory_rows, -1)]
    )
    cross_query_grad = lax.dot_general(
        normed_cross, grad_cross_queries, CONTRACT_FIRST, preferred_element_type=jnp.float32
    )
    cross_kv_grad = jnp.einsum(
        "md,cmh->dch", encoder, grad_cross_pair, preferred_element_type=jnp.float32
    )
    joined = model_sum(
        jnp.concatenate(
            [
                lax.dot_general(
                    grad_cross_queries,
                    cross_query,
                    CONTRACT_LAST,
                    preferred_element_type=jnp.float32,
                ),
                jnp.einsum(
                    "cmh,dch->md", grad_cross_pair, cross_kv, preferred_element_type=jnp.float32
                ),
            ],
            axis=0,
        )
    )
    grad_normed_cross = joined[:length]
    memory_grad = joined[length:]
    grad_from_cross, cross_gain_grad = norm_back(after_self, cross_gain, grad_normed_cross)
    grad_after_self = grad_after_cross + grad_from_cross
    grad_self_out = grad_after_self.astype(jnp.bfloat16)
    self_out_grad = lax.dot_general(
        grad_self_out, self_mix, CONTRACT_FIRST, preferred_element_type=jnp.float32
    )
    grad_self_mix = (
        jnp.dot(grad_self_out, self_out, preferred_element_type=jnp.float32)
        .astype(jnp.bfloat16)
        .reshape(length, heads_here, DH)
    )
    grad_queries, grad_keys, grad_values = attend_back(
        queries, key_value[0], key_value[1], allowed, self_total, grad_self_mix
    )
    grad_queries = grad_queries.reshape(length, -1)
    grad_pair = jnp.stack([grad_keys.reshape(length, -1), grad_values.reshape(length, -1)])
    self_query_grad = lax.dot_general(
        normed_self, grad_queries, CONTRACT_FIRST, preferred_element_type=jnp.float32
    )
    self_kv_grad = jnp.einsum(
        "td,cth->dch", normed_self, grad_pair, preferred_element_type=jnp.float32
    )
    grad_normed_self = model_sum(
        lax.dot_general(grad_queries, self_query, CONTRACT_LAST, preferred_element_type=jnp.float32)
        + jnp.einsum("cth,dch->td", grad_pair, self_kv, preferred_element_type=jnp.float32)
    )
    grad_from_self, self_gain_grad = norm_back(states, self_gain, grad_normed_self)
    grad_states = (grad_after_self + grad_from_self).astype(jnp.bfloat16)
    grad_every = lax.all_gather(
        lax.dynamic_slice_in_dim(grad_states, first_row, part_rows),
        ("dp", "mp"),
        axis=0,
        tiled=True,
    )
    own_start = (group_index * shards + shard_index) * own_rows
    offset_ids = ids_every - own_start
    target_row = jnp.where((offset_ids >= 0) & (offset_ids < own_rows), offset_ids, own_rows)
    embed_grad = jax.ops.segment_sum(
        grad_every.astype(jnp.float32), target_row, num_segments=own_rows + 1
    )[:own_rows]
    (
        self_query_grad,
        self_kv_grad,
        self_out_grad,
        self_gain_grad,
        cross_query_grad,
        cross_kv_grad,
        cross_out_grad,
        cross_gain_grad,
        ffn_in_grad,
        ffn_out_grad,
        ffn_gain_grad,
        final_gain_grad,
    ) = (
        lax.psum_scatter(self_query_grad, "dp", scatter_dimension=0, tiled=True),
        lax.psum_scatter(self_kv_grad, "dp", scatter_dimension=0, tiled=True),
        lax.psum_scatter(self_out_grad, "dp", scatter_dimension=0, tiled=True),
        lax.psum_scatter(self_gain_grad, "dp", scatter_dimension=0, tiled=True),
        lax.psum_scatter(cross_query_grad, "dp", scatter_dimension=0, tiled=True),
        lax.psum_scatter(cross_kv_grad, "dp", scatter_dimension=0, tiled=True),
        lax.psum_scatter(cross_out_grad, "dp", scatter_dimension=0, tiled=True),
        lax.psum_scatter(cross_gain_grad, "dp", scatter_dimension=0, tiled=True),
        lax.psum_scatter(ffn_in_grad, "dp", scatter_dimension=0, tiled=True),
        lax.psum_scatter(ffn_out_grad, "dp", scatter_dimension=0, tiled=True),
        lax.psum_scatter(ffn_gain_grad, "dp", scatter_dimension=0, tiled=True),
        lax.psum_scatter(final_gain_grad, "dp", scatter_dimension=0, tiled=True),
    )
    return (
        loss_value,
        memory_grad[None],
        embed_grad,
        head_grad,
        self_gain_grad,
        self_query_grad,
        self_kv_grad,
        self_out_grad,
        cross_gain_grad,
        cross_query_grad,
        cross_kv_grad,
        cross_out_grad,
        ffn_gain_grad,
        ffn_in_grad,
        ffn_out_grad,
        final_gain_grad,
    )


def solution(mesh):
    return jax.shard_map(
        on_device,
        mesh=mesh,
        in_specs=(
            P("dp", None),
            P("dp", None),
            P("dp", None),
            P("dp"),
            P("dp"),
            P("dp", None, None),
            P(("dp", "mp"), None),
            P(("dp", "mp"), None),
            P(),
            P(None, "mp"),
            P(None, None, "mp"),
            P(None, "mp"),
            P(),
            P(None, "mp"),
            P(None, None, "mp"),
            P(None, "mp"),
            P(),
            P(None, None, "mp"),
            P(None, "mp"),
            P(),
        ),
        out_specs=(
            P(),
            P("dp", None, None),
            P(("dp", "mp"), None),
            P(("dp", "mp"), None),
            P("dp"),
            P("dp", "mp"),
            P("dp", None, "mp"),
            P("dp", "mp"),
            P("dp"),
            P("dp", "mp"),
            P("dp", None, "mp"),
            P("dp", "mp"),
            P("dp"),
            P("dp", None, "mp"),
            P("dp", "mp"),
            P("dp"),
        ),
        check_vma=False,
    )
```

profile of v0, /device:TPU:0, one launch (start us, length us, event | category | flops | bytes accessed | tf_op | source)
XLA Modules:
  0.0 3112.3 jit_solution(15564806318175258070)
XLA Ops:
  10.4 71.4 %all-reduce.9 = (s32[8,4,32]{2,1,0:T(4,128)S(1)}, s32[1024]{0:T(1024)S(1)}) all-reduce(s32[8,4,32]{2,1,0:T(4,128)S(1)} %reshape.216, s32[1024]{0:T(1024)S(1)} %fusion.66), channel_id=1, replica_groups=mesh['dp'=8,'mp'=4] {'dp','mp'}, use_global_device_ids=true, to_apply=%add | all-reduce | flops 2048 | bytes 16384
  83.8 727.2 %all-gather.5.cloned.1.call-done = bf16[31264,768]{1,0:T(8,128)(2,1)} async-done(((bf16[7816,768]{1,0:T(8,128)(2,1)}), bf16[31264,768]{1,0:T(8,128)(2,1)}) %all-gather.5.cloned.1.call-update) | async-done | bytes 48021520 | tf_op jit(solution)/shard_map/all_gather | solution.py:126
  811.0 10.1 gather_fusion
  823.0 32.3 %reduce-scatter.15.cloned.1.call-done = f32[32,768]{1,0:T(8,128)} async-done(((f32[256,768]{1,0:T(8,128)}), f32[32,768]{1,0:T(8,128)}) %reduce-scatter.15.cloned.1.call-update) | async-done | bytes 98320 | tf_op jit(solution)/shard_map/reduce_scatter | solution.py:133
  856.3 13.7 all_gather.27
  878.4 35.3 %all-reduce.18.cloned.1.call-done = f32[128,768]{1,0:T(8,128)} async-done(((f32[128,768]{1,0:T(8,128)}), f32[128,768]{1,0:T(8,128)}) %all-reduce.18.cloned.1.call-update) | async-done | bytes 393232 | tf_op jit(solution)/shard_map/psum | solution.py:33
  917.8 36.8 %all-reduce.20.cloned.1.call-done = f32[128,768]{1,0:T(8,128)} async-done(((f32[128,768]{1,0:T(8,128)}), f32[128,768]{1,0:T(8,128)}) %all-reduce.20.cloned.1.call-update) | async-done | bytes 393232 | tf_op jit(solution)/shard_map/psum | solution.py:33
  960.8 35.4 %all-reduce.22.cloned.1.call-done = f32[128,768]{1,0:T(8,128)} async-done(((f32[128,768]{1,0:T(8,128)}), f32[128,768]{1,0:T(8,128)}) %all-reduce.22.cloned.1.call-update) | async-done | bytes 393232 | tf_op jit(solution)/shard_map/psum | solution.py:33
  997.9 9.3 all_gather.28
  1007.3 788.4 %all-gather.7.cloned.1.call-done = bf16[31264,768]{1,0:T(8,128)(2,1)} async-done(((bf16[7816,768]{1,0:T(8,128)(2,1)}), bf16[31264,768]{1,0:T(8,128)(2,1)}) %all-gather.7.cloned.1.call-update) | async-done | bytes 48021520 | tf_op jit(solution)/shard_map/all_gather | solution.py:127
  1795.7 31.8 %fusion.84 = (f32[256]{0:T(256)}, f32[256,31264]{0,1:T(8,128)}) fusion(bf16[256,768]{1,0:T(8,128)(2,1)S(1)} %all_gather.28, bf16[31264,768]{1,0:T(8,128)(2,1)} %all-gather.7.cloned.1.call-done), kind=kOutput, calls=%fused_computation.173 | convolution fusion | flops 12301508608 | bytes 80430080 | tf_op jit(solution)/shard_map/dot_general | solution.py:189
  1827.5 14.5 pmax.7
  1842.0 15.2 select_reduce_fusion
  1857.2 12.6 psum.66
  1871.1 28.7 fusion.78
  1899.9 31.4 %reduce-scatter.17.cloned.1.call-done = f32[32,768]{1,0:T(8,128)} async-done(((f32[256,768]{1,0:T(8,128)}), f32[32,768]{1,0:T(8,128)}) %reduce-scatter.17.cloned.1.call-update) | async-done | bytes 98320 | tf_op jit(solution)/shard_map/reduce_scatter | solution.py:207
  1932.2 13.6 all_gather.30
  1951.2 37.6 %all-reduce.24.cloned.1.call-done = f32[128,768]{1,0:T(8,128)} async-done(((f32[128,768]{1,0:T(8,128)}), f32[128,768]{1,0:T(8,128)}) %all-reduce.24.cloned.1.call-update) | async-done | bytes 393232 | tf_op jit(solution)/shard_map/psum | solution.py:33
  2002.3 55.6 %all-reduce.26.cloned.1.call-done = f32[384,768]{1,0:T(8,128)} async-done(((f32[384,768]{1,0:T(8,128)}), f32[384,768]{1,0:T(8,128)}) %all-reduce.26.cloned.1.call-update) | async-done | bytes 1179664 | tf_op jit(solution)/shard_map/psum | solution.py:33
  2070.6 2.4 fusion.25
  2073.1 2.7 copy.90
  2078.2 3.4 fusion.39
  2082.4 25.0 all-reduce.28.cloned.1.call-done
  2112.7 2.6 fusion.54
  2115.6 32.4 %convolution_convert_fusion = bf16[31264,768]{1,0:T(8,128)(2,1)} fusion(bf16[256,768]{1,0:T(8,128)(2,1)S(1)} %all_gather.28, f32[256,31264]{0,1:T(8,128)} %get-tuple-element.118, f32[256]{0:T(256)} %broadcast_select_fusion, f32[256]{0:T(256)} %copy-done.34, s32[256]{0:T(256)S(1)} %sub.143), kind=kOutput, calls=%fused_computation.2 | convolution fusion | flops 12365537280 | bytes 80432128 | tf_op jit(solution)/shard_map/dot_general | solution.py:215
  2149.2 807.6 %fusion = bf16[7840,768]{1,0:T(8,128)(2,1)} fusion(bf16[31264,768]{1,0:T(8,128)(2,1)} %convolution_convert_fusion), kind=kCustom, calls=%all-reduce-scatter | all-reduce-scatter fusion | flops 24084480 | bytes 60064256
  2961.6 50.7 %concatenate.4 = bf16[7912,768]{1,0:T(8,128)(2,1)} concatenate(bf16[72,768]{1,0:T(8,128)(2,1)S(1)} %collective-permute-done, bf16[7840,768]{1,0:T(8,128)(2,1)} %fusion), dimensions={0} | concatenate | bytes 24305664
  3013.6 13.9 dynamic-slice_convert_fusion
  3027.5 22.6 all-reduce.10
  3052.3 11.0 psum.68
  3071.3 17.8 scatter_custom_fusion
  3089.1 16.6 slice.54
  (269 shorter events, 84.5 us)
Async XLA Ops:
  7.2 948.5 %copy-start = (bf16[768,2,512]{2,1,0:T(2,128)(2,1)S(1)}, bf16[768,2,512]{2,1,0:T(2,128)(2,1)}, u32[]{:S(2)}) copy-start(bf16[768,2,512]{2,1,0:T(2,128)(2,1)} %param.37) | copy-start | bytes 4718596
  7.2 907.6 %copy-start.31 = (f32[768]{0:T(1024)S(1)}, f32[768]{0:T(1024)}, u32[]{:S(2)}) copy-start(f32[768]{0:T(1024)} %param.32) | copy-start | bytes 9220
  7.2 907.6 %copy-start.10 = (bf16[768,192]{0,1:T(8,128)(2,1)S(1)}, bf16[768,192]{0,1:T(8,128)(2,1)}, u32[]{:S(2)}) copy-start(bf16[768,192]{0,1:T(8,128)(2,1)} %param.33) | copy-start | bytes 884740
  7.2 909.5 %copy-start.11 = (bf16[768,192]{0,1:T(8,128)(2,1)S(1)}, bf16[768,192]{0,1:T(8,128)(2,1)}, u32[]{:S(2)}) copy-start(bf16[768,192]{0,1:T(8,128)(2,1)} %param.35) | copy-start | bytes 884740
  7.2 948.5 %copy-start.30 = (f32[768]{0:T(1024)S(1)}, f32[768]{0:T(1024)}, u32[]{:S(2)}) copy-start(f32[768]{0:T(1024)} %param.36) | copy-start | bytes 9220
  7.2 990.7 %copy-start.33 = (f32[768]{0:T(1024)S(1)}, f32[768]{0:T(1024)}, u32[]{:S(2)}) copy-start(f32[768]{0:T(1024)} %param.39) | copy-start | bytes 9220
  7.3 803.7 %all-gather.5.cloned.1.call-start = ((), (), s32[]{:S(2)}) async-start(), calls=%async_computation.10 | async-start | bytes 60026880 | tf_op jit(solution)/shard_map/all_gather | solution.py:126
  8.0 847.4 %reduce-scatter.15.cloned.1.call-start = ((), (), s32[]{:S(2)}) async-start(), calls=%async_computation.11 | async-start | bytes 884736 | tf_op jit(solution)/shard_map/reduce_scatter | solution.py:133
  822.1 91.5 %all-reduce.18.cloned.1.call-start = ((), (), s32[]{:S(2)}) async-start(), calls=%async_computation.12 | async-start | bytes 786432 | tf_op jit(solution)/shard_map/psum | solution.py:33
  869.9 127.6 %copy-start.2 = (bf16[128,768]{1,0:T(8,128)(2,1)}, bf16[128,768]{1,0:T(8,128)(2,1)S(1)}, u32[]{:S(2)}) copy-start(bf16[128,768]{1,0:T(8,128)(2,1)S(1)} %all_gather.27) | copy-start | bytes 589828
  876.1 78.5 %all-reduce.20.cloned.1.call-start = ((), (), s32[]{:S(2)}) async-start(), calls=%async_computation.13 | async-start | bytes 786432 | tf_op jit(solution)/shard_map/psum | solution.py:33
  917.7 78.5 %all-reduce.22.cloned.1.call-start = ((), (), s32[]{:S(2)}) async-start(), calls=%async_computation.14 | async-start | bytes 786432 | tf_op jit(solution)/shard_map/psum | solution.py:33
  959.4 836.3 %all-gather.7.cloned.1.call-start = ((), (), s32[]{:S(2)}) async-start(), calls=%async_computation.15 | async-start | bytes 60026880 | tf_op jit(solution)/shard_map/all_gather | solution.py:127
  960.0 971.3 %reduce-scatter.17.cloned.1.call-start = ((), (), s32[]{:S(2)}) async-start(), calls=%async_computation.16 | async-start | bytes 884736 | tf_op jit(solution)/shard_map/reduce_scatter | solution.py:207
  1899.8 176.1 %copy-start.32 = (f32[768]{0:T(1024)S(1)}, f32[768]{0:T(1024)}, u32[]{:S(2)}) copy-start(f32[768]{0:T(1024)} %param.28) | copy-start | bytes 9220
  1899.8 89.0 %all-reduce.24.cloned.1.call-start = ((), (), s32[]{:S(2)}) async-start(), calls=%async_computation.17 | async-start | bytes 786432 | tf_op jit(solution)/shard_map/psum | solution.py:33
  1951.2 161.5 %copy-start.6 = (bf16[128,768]{1,0:T(8,128)(2,1)S(1)}, bf16[128,768]{1,0:T(8,128)(2,1)}, u32[]{:S(2)}) copy-start(bf16[128,768]{1,0:T(8,128)(2,1)} %copy-done.5) | copy-start | bytes 589828
  1951.2 106.7 %all-reduce.26.cloned.1.call-start = ((), (), s32[]{:S(2)}) async-start(), calls=%async_computation.18 | async-start | bytes 2359296 | tf_op jit(solution)/shard_map/psum | solution.py:33
  2002.2 105.2 %all-reduce.28.cloned.1.call-start = ((), (), s32[]{:S(2)}) async-start(), calls=%async_computation.19 | async-start | bytes 786432 | tf_op jit(solution)/shard_map/psum | solution.py:33
  2070.6 995.1 %reduce-scatter.33.cloned.1.call-start = ((), (), s32[]{:S(2)}) async-start(), calls=%async_computation.28 | async-start | bytes 1327104
  2075.8 991.7 %reduce-scatter.21.cloned.1.call-start = ((), (), s32[]{:S(2)}) async-start(), calls=%async_computation.22 | async-start | bytes 1769472 | tf_op jit(solution)/shard_map/reduce_scatter | solution.py:333
  2078.2 991.1 %reduce-scatter.29.cloned.1.call-start = ((), (), s32[]{:S(2)}) async-start(), calls=%async_computation.26 | async-start | bytes 3538944 | tf_op jit(solution)/shard_map/reduce_scatter | solution.py:340
  2081.6 989.7 %all-gather.9.cloned.1.call-start = ((), (), s32[]{:S(2)}) async-start(), calls=%async_computation.20 | async-start | bytes 1622016 | tf_op jit(solution)/shard_map/all_gather | solution.py:306
  2109.4 996.3 %reduce-scatter.25.cloned.1.call-start = ((), (), s32[]{:S(2)}) async-start(), calls=%async_computation.24 | async-start | bytes 884736 | tf_op jit(solution)/shard_map/reduce_scatter | solution.py:336
  2111.4 994.3 %reduce-scatter.27.cloned.1.call-start = ((), (), s32[]{:S(2)}) async-start(), calls=%async_computation.25 | async-start | bytes 884736 | tf_op jit(solution)/shard_map/reduce_scatter | solution.py:338
  2112.6 993.1 %reduce-scatter.31.cloned.1.call-start = ((), (), s32[]{:S(2)}) async-start(), calls=%async_computation.27 | async-start | bytes 1769472 | tf_op jit(solution)/shard_map/reduce_scatter | solution.py:341
  2115.3 990.4 %reduce-scatter.23.cloned.1.call-start = ((), (), s32[]{:S(2)}) async-start(), calls=%async_computation.23 | async-start | bytes 884736 | tf_op jit(solution)/shard_map/reduce_scatter | solution.py:334
  2149.2 809.9 %copy-start.43 = (s32[1024]{0:T(1024)S(1)}, s32[1024]{0:T(1024)}, u32[]{:S(2)}) copy-start(s32[1024]{0:T(1024)} %copy-done.42) | copy-start | bytes 12292
  2149.2 809.9 %copy-start.52 = (u32[32]{0:T(128)S(1)}, u32[32]{0:T(128)}, u32[]{:S(2)}) copy-start(u32[32]{0:T(128)} %constant.103) | copy-start | bytes 388
  2149.2 810.5 %copy-start.55 = (u32[32]{0:T(128)S(1)}, u32[32]{0:T(128)}, u32[]{:S(2)}) copy-start(u32[32]{0:T(128)} %constant.107) | copy-start | bytes 388
  2149.2 956.5 %reduce-scatter.19.cloned.1.call-start = ((), (), s32[]{:S(2)}) async-start(), calls=%async_computation.21 | async-start | bytes 884736 | tf_op jit(solution)/shard_map/reduce_scatter | solution.py:332
  2957.8 3.8 collective-permute-start
  (44 other events, 1245.3 us)
Sparse Core Ops, SparseCore 0:
  9.7 801.2 all-gather.4
  822.3 33.0 reduce-scatter.14
  876.2 37.4 all-reduce.17
  917.8 36.6 all-reduce.19
  959.5 36.6 all-reduce.21
  997.8 797.8 all-gather.6
  1899.9 31.3 reduce-scatter.16
  1951.3 37.4 all-reduce.23
  2002.3 55.5 all-reduce.25
  2070.7 36.6 all-reduce.27
  2111.0 36.3 reduce-scatter.32
  2150.5 38.4 reduce-scatter.20
  2192.4 46.2 reduce-scatter.28
  2241.8 57.7 all-gather.8
  2303.5 34.6 reduce-scatter.24
  2342.1 34.9 reduce-scatter.26
  2381.2 38.4 reduce-scatter.30
  2423.6 34.9 reduce-scatter.22
  3013.7 33.1 reduce-scatter.18
where the time goes:
time: 3120 us; the launch traced here: 3110 us
  waiting for transfers between devices  1810 us (58%)
  blocking collectives  976 us (31%)
  matrix products  140 us (4%)
  local copies, waits for them, and re-layouts  98.2 us (3%)
  other arithmetic  70.1 us (2%)
    unnamed x2, blocking collectives  879 us
    all_gather x1, waiting for transfers between devices, on_device(): lax.all_gather(head_table, 'mp', axis=0, tiled=True)  788 us
    all_gather x1, waiting for transfers between devices, on_device(): lax.all_gather(embed_table, 'mp', axis=0, tiled=True)  727 us
    psum x6, waiting for transfers between devices, model_sum(): return lax.psum(values, 'mp')  226 us
    unnamed x129, local copies, waits for them, and re-layouts  68.7 us
  transfers between devices with their start and end apart: 20, of which 10 were waited for; matrix products, arithmetic and copies ran while one was open for 31% of the time, Pallas kernels for 0%

commit v1 on v0

v1 whole, which is shorter than its diff:
```python
import jax
import jax.numpy as jnp
from jax import lax
from jax.sharding import PartitionSpec as P

DH = 64

EPSILON = 1e-06
NEGATIVE = -1e30
CONTRACT_FIRST = (((0,), (0,)), ((), ()))
CONTRACT_LAST = (((1,), (1,)), ((), ()))
BF = jnp.bfloat16
F32 = jnp.float32


def normed(values, gain):
    scale_rows = lax.rsqrt(jnp.mean(values * values, axis=-1, keepdims=True) + EPSILON)
    return values * scale_rows * gain


def norm_back(values, gain, upstream):
    scale_rows = lax.rsqrt(jnp.mean(values * values, axis=-1, keepdims=True) + EPSILON)
    weighted = upstream * gain
    inner_mean = jnp.mean(values * weighted, axis=-1, keepdims=True)
    grad_values = scale_rows * weighted - values * scale_rows * scale_rows * scale_rows * inner_mean
    return (grad_values, jnp.sum(upstream * values * scale_rows, axis=0))


def gelu_tanh(values):
    return jax.nn.gelu(values, approximate=True)


def swap(values, axis, distance):
    size = lax.axis_size(axis)
    return lax.ppermute(values, axis, [(i, i ^ distance) for i in range(size)])


def model_scatter(blocks):
    total = blocks[0].astype(F32)
    sent = blocks.astype(BF)
    for k in range(1, blocks.shape[0]):
        total = total + swap(sent[k], "mp", k).astype(F32)
    return total


def model_gather(own):
    shards = lax.axis_size("mp")
    return jnp.stack([own] + [swap(own, "mp", k) for k in range(1, shards)])


def bit_orders(size):
    bits = [1 << b for b in range(1, size.bit_length() - 1)]
    return bits, bits[::-1]


def group_gather(own):
    size = lax.axis_size("dp")
    half = own.shape[0] // 2
    orders = bit_orders(size)
    parts = []
    for order, piece in zip(orders, (own[:half], own[half:])):
        held = {0: piece}
        parts.append(held)
    for step in range(len(orders[0])):
        for order, held in zip(orders, parts):
            bit = order[step]
            keys = sorted(held)
            got = swap(jnp.stack([held[g] for g in keys]), "dp", bit)
            for place, g in enumerate(keys):
                held[g ^ bit] = got[place]
    keys = sorted(parts[0])
    here = jnp.stack([jnp.concatenate([parts[0][g], parts[1][g]]) for g in keys])
    there = swap(here, "dp", 1)
    every = dict(zip(keys, here)) | {g ^ 1: there[place] for place, g in enumerate(keys)}
    return jnp.stack([every[g] for g in range(size)])


def group_scatter(blocks, merge):
    size = blocks[0].shape[0]
    half = blocks[0].shape[1] // 2
    even, odd = list(range(0, size, 2)), list(range(1, size, 2))
    sent = [jnp.stack([b[g] for g in odd]) for b in blocks]
    kept = tuple(jnp.stack([b[g] for g in even]) for b in blocks)
    kept = merge(kept, tuple(swap(s, "dp", 1) for s in sent))
    orders = bit_orders(size)
    parts = []
    for side in range(2):
        parts.append(
            (list(even), tuple(b[:, side * half : (side + 1) * half] for b in kept))
        )
    for step in range(len(orders[0])):
        for side, order in enumerate(orders):
            bit = order[step]
            keys, held = parts[side]
            stay = [i for i, g in enumerate(keys) if not g & bit]
            go = [keys.index(keys[i] ^ bit) for i in stay]
            sent = tuple(jnp.stack([b[i] for i in go]) for b in held)
            mine = tuple(jnp.stack([b[i] for i in stay]) for b in held)
            parts[side] = (
                [keys[i] for i in stay],
                merge(mine, tuple(swap(s, "dp", bit) for s in sent)),
            )
    return tuple(
        jnp.concatenate([a[0], b[0]]) for a, b in zip(parts[0][1], parts[1][1])
    )


def add_merge(mine, other):
    return tuple(a + b for a, b in zip(mine, other))


def soft_merge(mine, other):
    (values_a, total_a), (values_b, total_b) = mine, other
    total = jnp.logaddexp(total_a, total_b)
    values = values_a.astype(F32) * jnp.exp(total_a - total)[..., None] + values_b.astype(
        F32
    ) * jnp.exp(total_b - total)[..., None]
    return (values.astype(BF), total)


def rows_scatter(values):
    size, index = lax.axis_size("dp"), lax.axis_index("dp")
    rows, columns = values.shape
    values = values.astype(BF).reshape(size // 2, 2, rows // size, columns)
    mine = lax.dynamic_index_in_dim(values, index & 1, 1, keepdims=False)
    sent = lax.dynamic_index_in_dim(values, 1 - (index & 1), 1, keepdims=False)
    mine = (mine.astype(F32) + swap(sent, "dp", 1).astype(F32)).astype(BF)
    orders = bit_orders(size)
    half = columns // 2
    parts = [mine[..., :half], mine[..., half:]]
    left = [list(orders[0]), list(orders[0])]
    for step in range(len(orders[0])):
        for side, order in enumerate(orders):
            bit = order[step]
            held = parts[side]
            low = 1
            for other in left[side]:
                if other < bit:
                    low *= 2
            left[side].remove(bit)
            held = held.reshape((held.shape[0] // (2 * low), 2, low) + held.shape[1:])
            own_bit = (index // bit) & 1
            keep = lax.dynamic_index_in_dim(held, own_bit, 1, keepdims=False)
            sent = lax.dynamic_index_in_dim(held, 1 - own_bit, 1, keepdims=False)
            total = keep.astype(F32) + swap(sent, "dp", bit).astype(F32)
            total = total.reshape((total.shape[0] * low,) + total.shape[2:])
            parts[side] = total if step == len(orders[0]) - 1 else total.astype(BF)
    return jnp.concatenate([parts[0][0], parts[1][0]], axis=-1).astype(F32)


def attend(queries, key_rows, value_rows, allowed):
    scores = jnp.einsum("qhe,khe->hqk", queries, key_rows, preferred_element_type=F32)
    scores = jnp.where(allowed, scores, NEGATIVE)
    top_score = jnp.max(scores, axis=-1, keepdims=True)
    log_total = top_score + jnp.log(jnp.sum(jnp.exp(scores - top_score), axis=-1, keepdims=True))
    weights = jnp.exp(scores - log_total).astype(BF)
    mixed = jnp.einsum("hqk,khe->qhe", weights, value_rows, preferred_element_type=F32)
    return (mixed.astype(BF), log_total)


def attend_back(queries, key_rows, value_rows, allowed, log_total, upstream):
    scores = jnp.einsum("qhe,khe->hqk", queries, key_rows, preferred_element_type=F32)
    scores = jnp.where(allowed, scores, NEGATIVE)
    probs = jnp.exp(scores - log_total)
    weights = probs.astype(BF)
    pulled = jnp.einsum("qhe,khe->hqk", upstream, value_rows, preferred_element_type=F32)
    grad_scores = (probs * (pulled - jnp.sum(probs * pulled, axis=-1, keepdims=True))).astype(BF)
    grad_queries = jnp.einsum(
        "hqk,khe->qhe", grad_scores, key_rows, preferred_element_type=F32
    ).astype(BF)
    grad_keys = jnp.einsum(
        "hqk,qhe->khe", grad_scores, queries, preferred_element_type=F32
    ).astype(BF)
    grad_values = jnp.einsum(
        "hqk,qhe->khe", weights, upstream, preferred_element_type=F32
    ).astype(BF)
    return (grad_queries, grad_keys, grad_values)


def on_device(
    token_ids,
    target_ids,
    segment_ids,
    target_length,
    memory_length,
    memory,
    embed_table,
    head_table,
    self_gain,
    self_query,
    self_kv,
    self_out,
    cross_gain,
    cross_query,
    cross_kv,
    cross_out,
    ffn_gain,
    ffn_in,
    ffn_out,
    final_gain,
):
    groups = lax.axis_size("dp")
    shards = lax.axis_size("mp")
    group_index = lax.axis_index("dp")
    shard_index = lax.axis_index("mp")
    length = token_ids.shape[1]
    part_rows = length // shards
    own_rows, width = embed_table.shape
    memory_rows = memory.shape[1]
    heads_here = self_query.shape[1] // DH
    tokens = groups * length
    loss_scale = 1.0 / tokens
    own_start = (group_index * shards + shard_index) * own_rows

    shard_order = shard_index ^ jnp.arange(shards)
    group_order = group_index ^ jnp.arange(groups)

    def relative(row):
        return row.reshape(shards, part_rows)[shard_order].reshape(length)

    positions = relative(jnp.arange(length))
    segments = relative(segment_ids[0])
    marked = jnp.where(positions < target_length[0], relative(target_ids[0]), -1)
    ids_here = relative(token_ids[0])
    both = lax.all_gather(jnp.stack([ids_here, marked]), "dp", axis=0)[group_order]
    ids_every = both[:, 0].reshape(tokens)
    marked_every = both[:, 1].reshape(tokens)

    def look_up(table, ids):
        local = ids - own_start
        inside = (local >= 0) & (local < own_rows)
        rows = jnp.take(table, jnp.clip(local, 0, own_rows - 1), axis=0)
        rows = jnp.where(inside[:, None], rows, jnp.zeros((), BF))
        (mine,) = group_scatter((rows.reshape(groups, length, width),), add_merge)
        return model_scatter(mine.reshape(shards, part_rows, width))

    def spread(own):
        return model_gather(own.astype(BF)).reshape(length, width)

    def gather_sum(partial):
        return model_scatter(partial.reshape(shards, part_rows, width))

    states = look_up(embed_table, ids_every)
    normed_self = spread(normed(states, self_gain))
    queries = (
        jnp.dot(normed_self, self_query, preferred_element_type=F32)
        .astype(BF)
        .reshape(length, heads_here, DH)
    )
    key_value = (
        jnp.einsum("td,dch->cth", normed_self, self_kv, preferred_element_type=F32)
        .astype(BF)
        .reshape(2, length, heads_here, DH)
    )
    allowed = (positions[:, None] >= positions[None, :]) & (segments[:, None] == segments[None, :])
    self_mix, self_total = attend(queries, key_value[0], key_value[1], allowed)
    self_mix = self_mix.reshape(length, -1)
    after_self = states + gather_sum(
        lax.dot_general(self_mix, self_out, CONTRACT_LAST, preferred_element_type=F32)
    )
    encoder = memory[0]
    normed_cross = spread(normed(after_self, cross_gain))
    cross_queries = (
        jnp.dot(normed_cross, cross_query, preferred_element_type=F32)
        .astype(BF)
        .reshape(length, heads_here, DH)
    )
    cross_pair = (
        jnp.einsum("md,dch->cmh", encoder, cross_kv, preferred_element_type=F32)
        .astype(BF)
        .reshape(2, memory_rows, heads_here, DH)
    )
    reachable = (jnp.arange(memory_rows) < memory_length[0])[None, :]
    cross_mix, cross_total = attend(cross_queries, cross_pair[0], cross_pair[1], reachable)
    cross_mix = cross_mix.reshape(length, -1)
    after_cross = after_self + gather_sum(
        lax.dot_general(cross_mix, cross_out, CONTRACT_LAST, preferred_element_type=F32)
    )
    normed_ffn = spread(normed(after_cross, ffn_gain))
    inner_pre = jnp.einsum("td,dcf->ctf", normed_ffn, ffn_in, preferred_element_type=F32)
    up_pre = inner_pre[1]
    activated, gelu_pull = jax.vjp(gelu_tanh, inner_pre[0])
    hidden = (activated * up_pre).astype(BF)
    after_ffn = after_cross + gather_sum(
        lax.dot_general(hidden, ffn_out, CONTRACT_LAST, preferred_element_type=F32)
    )
    final_own = normed(after_ffn, final_gain).astype(BF)
    final_every = group_gather(spread(final_own)).reshape(tokens, width)
    target_rows = look_up(head_table, marked_every)

    logits = lax.dot_general(final_every, head_table, CONTRACT_LAST, preferred_element_type=F32)
    target_hit = jnp.arange(own_rows)[None, :] == (marked_every - own_start)[:, None]
    peak = jnp.max(logits, axis=1)
    raised = jnp.exp(logits - peak[:, None])
    share = jnp.sum(raised, axis=1)
    probs = jnp.where(target_hit, 0.0, raised).astype(BF)
    pulled = jnp.dot(probs, head_table, preferred_element_type=F32) / share[:, None]
    pulled, totals = group_scatter(
        (
            pulled.astype(BF).reshape(groups, length, width),
            (peak + jnp.log(share)).reshape(groups, length),
        ),
        soft_merge,
    )
    pulled = pulled.reshape(shards, part_rows, width)
    totals = totals.reshape(shards, part_rows)
    parts = [(pulled[0], totals[0])] + [
        (swap(pulled[k], "mp", k), swap(totals[k], "mp", k)) for k in range(1, shards)
    ]
    log_total = jax.nn.logsumexp(jnp.stack([t for _, t in parts]), axis=0)
    grad_final = sum(v.astype(F32) * jnp.exp(t - log_total)[:, None] for v, t in parts)
    chosen = jnp.sum(final_own.astype(F32) * target_rows, axis=1)
    keep_own = (marked[:part_rows] >= 0).astype(F32) * loss_scale
    missing = jnp.exp(chosen - log_total) - 1.0
    grad_final = (grad_final + missing[:, None] * target_rows) * keep_own[:, None]

    both = jnp.stack([log_total, missing, (log_total - chosen) * keep_own], axis=1)
    both = model_gather(both).reshape(length, 3)
    both = group_gather(both).reshape(tokens, 3)
    lines = jnp.sum(both[:, 2].reshape(groups, shards, part_rows), axis=-1)
    loss_value = jnp.sum(lines[group_order][:, shard_order])
    keep_every = (marked_every >= 0).astype(F32) * loss_scale
    factor = jnp.exp(peak - both[:, 0]) * keep_every
    grad_logits = jnp.where(
        target_hit, (both[:, 1] * keep_every)[:, None], probs.astype(F32) * factor[:, None]
    ).astype(BF)
    head_grad = lax.dot_general(
        grad_logits, final_every, CONTRACT_FIRST, preferred_element_type=F32
    )

    grad_after_ffn, final_gain_grad = norm_back(after_ffn, final_gain, grad_final)
    grad_down = spread(grad_after_ffn)
    ffn_out_grad = lax.dot_general(grad_down, hidden, CONTRACT_FIRST, preferred_element_type=F32)
    grad_hidden = jnp.dot(grad_down, ffn_out, preferred_element_type=F32)
    grad_gate = gelu_pull(grad_hidden * up_pre)[0]
    grad_inner = jnp.stack([grad_gate, grad_hidden * activated]).astype(BF)
    ffn_in_grad = jnp.einsum("td,ctf->dcf", normed_ffn, grad_inner, preferred_element_type=F32)
    grad_normed_ffn = gather_sum(
        jnp.einsum("ctf,dcf->td", grad_inner, ffn_in, preferred_element_type=F32)
    )
    grad_from_ffn, ffn_gain_grad = norm_back(after_cross, ffn_gain, grad_normed_ffn)
    grad_after_cross = grad_after_ffn + grad_from_ffn
    grad_cross_out = spread(grad_after_cross)
    cross_out_grad = lax.dot_general(
        grad_cross_out, cross_mix, CONTRACT_FIRST, preferred_element_type=F32
    )
    grad_cross_mix = (
        jnp.dot(grad_cross_out, cross_out, preferred_element_type=F32)
        .astype(BF)
        .reshape(length, heads_here, DH)
    )
    grad_cross_queries, grad_cross_keys, grad_cross_values = attend_back(
        cross_queries, cross_pair[0], cross_pair[1], reachable, cross_total, grad_cross_mix
    )
    grad_cross_queries = grad_cross_queries.reshape(length, -1)
    grad_cross_pair = jnp.stack(
        [grad_cross_keys.reshape(memory_rows, -1), grad_cross_values.reshape(memory_rows, -1)]
    )
    cross_query_grad = lax.dot_general(
        normed_cross, grad_cross_queries, CONTRACT_FIRST, preferred_element_type=F32
    )
    cross_kv_grad = jnp.einsum("md,cmh->dch", encoder, grad_cross_pair, preferred_element_type=F32)
    grad_normed_cross = gather_sum(
        lax.dot_general(grad_cross_queries, cross_query, CONTRACT_LAST, preferred_element_type=F32)
    )
    memory_part = model_scatter(
        jnp.einsum("cmh,dch->md", grad_cross_pair, cross_kv, preferred_element_type=F32).reshape(
            shards, memory_rows // shards, width
        )[shard_order]
    )
    memory_grad = model_gather(memory_part.astype(BF))[shard_order].reshape(memory_rows, width)
    memory_grad = memory_grad.astype(F32)
    grad_from_cross, cross_gain_grad = norm_back(after_self, cross_gain, grad_normed_cross)
    grad_after_self = grad_after_cross + grad_from_cross
    grad_self_out = spread(grad_after_self)
    self_out_grad = lax.dot_general(
        grad_self_out, self_mix, CONTRACT_FIRST, preferred_element_type=F32
    )
    grad_self_mix = (
        jnp.dot(grad_self_out, self_out, preferred_element_type=F32)
        .astype(BF)
        .reshape(length, heads_here, DH)
    )
    grad_queries, grad_keys, grad_values = attend_back(
        queries, key_value[0], key_value[1], allowed, self_total, grad_self_mix
    )
    grad_queries = grad_queries.reshape(length, -1)
    grad_pair = jnp.stack([grad_keys.reshape(length, -1), grad_values.reshape(length, -1)])
    self_query_grad = lax.dot_general(
        normed_self, grad_queries, CONTRACT_FIRST, preferred_element_type=F32
    )
    self_kv_grad = jnp.einsum("td,cth->dch", normed_self, grad_pair, preferred_element_type=F32)
    grad_normed_self = gather_sum(
        lax.dot_general(grad_queries, self_query, CONTRACT_LAST, preferred_element_type=F32)
        + jnp.einsum("cth,dch->td", grad_pair, self_kv, preferred_element_type=F32)
    )
    grad_from_self, self_gain_grad = norm_back(states, self_gain, grad_normed_self)
    grad_states = (grad_after_self + grad_from_self).astype(BF)
    grad_every = group_gather(spread(grad_states)).reshape(tokens, width)
    hits = (jnp.arange(own_rows)[:, None] == (ids_every - own_start)[None, :]).astype(BF)
    embed_grad = jnp.dot(hits, grad_every, preferred_element_type=F32)

    def weight_sums(pieces):
        flat = [p.reshape(p.shape[0], -1) for p in pieces]
        summed = rows_scatter(jnp.concatenate(flat, axis=1))
        results, at = [], 0
        for piece, line in zip(pieces, flat):
            part = summed[:, at : at + line.shape[1]]
            results.append(part.reshape((part.shape[0],) + piece.shape[1:]))
            at += line.shape[1]
        return results

    ffn_in_grad, ffn_out_grad = weight_sums([ffn_in_grad, ffn_out_grad])
    cross_query_grad, cross_kv_grad, cross_out_grad = weight_sums(
        [cross_query_grad, cross_kv_grad, cross_out_grad]
    )
    self_query_grad, self_kv_grad, self_out_grad = weight_sums(
        [self_query_grad, self_kv_grad, self_out_grad]
    )
    gains = jnp.stack([self_gain_grad, cross_gain_grad, ffn_gain_grad, final_gain_grad])
    gains = gains + sum(swap(gains, "mp", k) for k in range(1, shards))
    gains = gains.reshape(4, groups, width // groups)[:, group_order].transpose(1, 0, 2)
    gains = gains[0] + sum(swap(gains[g], "dp", g) for g in range(1, groups))
    return (
        loss_value,
        memory_grad[None],
        embed_grad,
        head_grad,
        gains[0],
        self_query_grad,
        self_kv_grad,
        self_out_grad,
        gains[1],
        cross_query_grad,
        cross_kv_grad,
        cross_out_grad,
        gains[2],
        ffn_in_grad,
        ffn_out_grad,
        gains[3],
    )


def solution(mesh):
    return jax.shard_map(
        on_device,
        mesh=mesh,
        in_specs=(
            P("dp", None),
            P("dp", None),
            P("dp", None),
            P("dp"),
            P("dp"),
            P("dp", None, None),
            P(("dp", "mp"), None),
            P(("dp", "mp"), None),
            P(),
            P(None, "mp"),
            P(None, None, "mp"),
            P(None, "mp"),
            P(),
            P(None, "mp"),
            P(None, None, "mp"),
            P(None, "mp"),
            P(),
            P(None, None, "mp"),
            P(None, "mp"),
            P(),
        ),
        out_specs=(
            P(),
            P("dp", None, None),
            P(("dp", "mp"), None),
            P(("dp", "mp"), None),
            P("dp"),
            P("dp", "mp"),
            P("dp", None, "mp"),
            P("dp", "mp"),
            P("dp"),
            P("dp", "mp"),
            P("dp", None, "mp"),
            P("dp", "mp"),
            P("dp"),
            P("dp", None, "mp"),
            P("dp", "mp"),
            P("dp"),
        ),
        check_vma=False,
    )
```

time: 3120 us -> 529 us (0.17)
  waiting for transfers between devices: 1810 us -> 101 us
  blocking collectives: 976 us -> 10.4 us
  starting transfers between devices: 2.29 us -> 145 us
    all_gather x3 -> x0, waiting for transfers between devices: 1520 us -> none  [the longest x1 788 us: on_device(): lax.all_gather(head_table, 'mp', axis=0, tiled=True)]
    unnamed x2 -> x0, blocking collectives: 879 us -> none
    psum x6 -> x0, waiting for transfers between devices: 226 us -> none  [model_sum(): return lax.psum(values, 'mp')]
    ppermute x0 -> x123, starting transfers between devices: none -> 145 us  [swap(): return lax.ppermute(values, axis, [(i, i ^ distance) for i in range(size)])]
    ppermute x0 -> x123, waiting for transfers between devices: none -> 101 us  [swap(): return lax.ppermute(values, axis, [(i, i ^ distance) for i in range(size)])]
    reduce_scatter x9 -> x0, waiting for transfers between devices: 63.8 us -> none  [the longest x1 32.3 us: on_device(): lax.psum_scatter(jnp.where(inside[:, None], looked.astype(jnp.float32), 0...]
    unnamed x129 -> x286, local copies, waits for them, and re-layouts: 68.7 us -> 10.8 us
    psum x3 -> x0, blocking collectives: 46.2 us -> none  [the longest x2 35.2 us: on_device(): lax.psum((jnp.sum(jnp.exp(logits - peak_logit[:, None]), axis=1), chosen)...]
  transfers between devices with their start and end apart: 20 -> 123, of which waited for: 10 -> 60; matrix products, arithmetic and copies ran while one was open for 31% -> 27% of each run, Pallas kernels for 0% -> 0%
where the time goes in v1:
time: 529 us; the launch traced here: 522 us
  starting transfers between devices  145 us (27%)
  matrix products  110 us (21%)
  waiting for transfers between devices  101 us (19%)
  local copies, waits for them, and re-layouts  76.6 us (14%)
  other arithmetic  74.4 us (14%)
  blocking collectives  10.4 us (2%)
    ppermute x123, starting transfers between devices, swap(): return lax.ppermute(values, axis, [(i, i ^ distance) for i in range(size)])  145 us
    ppermute x123, waiting for transfers between devices, swap(): return lax.ppermute(values, axis, [(i, i ^ distance) for i in range(size)])  101 us
    dot_general x1, matrix products, on_device(): lax.dot_general(grad_logits, final_every, CONTRACT_FIRST, preferred_eleme...  26.6 us
    dot_general x1, matrix products, on_device(): lax.dot_general(final_every, head_table, CONTRACT_LAST, preferred_element...  21.6 us
    dot_general x1, matrix products, on_device(): jnp.dot(probs, head_table, preferred_element_type=F32) / share[:, None]  21.2 us
    gather x2, local copies, waits for them, and re-layouts, look_up(): rows = jnp.take(table, jnp.clip(local, 0, own_rows - 1), axis=0)  20.9 us
    dot_general x1, matrix products, on_device(): embed_grad = jnp.dot(hits, grad_every, preferred_element_type=F32)  18.1 us
    reduce_sum x1, other arithmetic, on_device(): share = jnp.sum(raised, axis=1)  14.7 us
  transfers between devices with their start and end apart: 123, of which 60 were waited for; matrix products, arithmetic and copies ran while one was open for 27% of the time, Pallas kernels for 0%

profile of v1, /device:TPU:0, one launch (start us, length us, event | category | flops | bytes accessed | tf_op | source)
XLA Modules:
  0.0 522.3 jit_solution(5783441444771854143)
XLA Ops:
  6.6 10.4 %all-gather.1 = s32[8,2,128]{2,1,0:T(2,128)S(1)} all-gather(s32[1,2,128]{2,1,0:T(2,128)S(1)} %add_bitcast_fusion.6), channel_id=2, replica_groups=mesh['dp'=8,'mp'=4] {'dp'}, dimensions={0}, use_global_device_ids=true | all-gather | bytes 9216 | tf_op jit(solution)/shard_map/all_gather | solution.py:225
  18.2 10.4 %gather_fusion.10 = bf16[1024,768]{1,0:T(8,128)(2,1)S(1)} fusion(bf16[7816,768]{1,0:T(8,128)(2,1)} %param.28, s32[1024]{0:T(1024)S(1)} %get-tuple-element.215), kind=kCustom, calls=%fused_computation.clone | custom fusion | bytes 3149824 | tf_op jit(solution)/shard_map/jit(_take)/gather | solution.py:232
  31.6 10.4 %gather_fusion.11 = bf16[1024,768]{1,0:T(8,128)(2,1)S(1)} fusion(bf16[7816,768]{1,0:T(8,128)(2,1)} %param.29, s32[1024]{0:T(1024)S(1)} %get-tuple-element.216), kind=kCustom, calls=%fused_computation.1.clone | custom fusion | bytes 3149824 | tf_op jit(solution)/shard_map/jit(_take)/gather | solution.py:232
  70.0 2.7 collective-permute-start.6
  72.9 3.2 collective-permute-done.6
  80.0 3.4 collective-permute-start.10
  87.7 3.9 collective-permute-start.12
  93.7 4.1 collective-permute-done.13
  99.5 3.1 collective-permute-start.16
  111.8 3.0 collective-permute-done.18
  118.6 2.8 collective-permute-start.22
  138.2 2.9 collective-permute-start.28
  151.1 3.5 collective-permute-done.31
  165.3 21.6 %fusion.159 = (f32[1024]{0:T(1024)S(1)}, f32[1024,7816]{0,1:T(8,128)}) fusion(bf16[1024,768]{1,0:T(8,128)(2,1)S(1)} %bitcast.766, bf16[7816,768]{1,0:T(8,128)(2,1)} %param.29), kind=kOutput, calls=%fused_computation.494 | convolution fusion | flops 12301507584 | bytes 45596672 | tf_op jit(solution)/shard_map/dot_general | solution.py:291
  186.9 14.7 %fusion.1 = f32[1024]{0:T(1024)S(1)} fusion(f32[1024,7816]{0,1:T(8,128)} %get-tuple-element.202, f32[1024]{0:T(1024)S(1)} %get-tuple-element.201), kind=kLoop, calls=%fused_computation.18 | loop fusion | flops 16006144 | bytes 32022528 | tf_op jit(solution)/shard_map/reduce_sum | solution.py:295
  201.6 21.2 %divide_convert_fusion = bf16[1024,768]{1,0:T(8,128)(2,1)} fusion(bf16[7816,768]{1,0:T(8,128)(2,1)} %param.29, f32[1024]{0:T(1024)S(1)} %fusion.1, f32[1024,7816]{0,1:T(8,128)} %get-tuple-element.202, s32[1024]{0:T(1024)S(1)} %bitcast.762, f32[1024]{0:T(1024)S(1)} %get-tuple-element.201), kind=kOutput, calls=%fused_computation.24 | convolution fusion | flops 12327092224 | bytes 45604864 | tf_op jit(solution)/shard_map/dot_general | solution.py:297
  249.1 2.7 collective-permute-done.52
  265.4 4.9 collective-permute-done.59
  289.4 26.6 %fusion.2 = f32[7816,768]{1,0:T(8,128)} fusion(bf16[1024,768]{1,0:T(8,128)(2,1)S(1)} %bitcast.767, f32[1024]{0:T(1024)S(1)} %bitcast.779, f32[1024]{0:T(1024)S(1)} %bitcast.778, s32[1024]{0:T(1024)S(1)} %bitcast.763, f32[1024,7816]{0,1:T(8,128)} %get-tuple-element.202, f32[1024]{0:T(1024)S(1)} %get-tuple-element.201), kind=kOutput, calls=%fused_computation.19 | convolution fusion | flops 12349530112 | bytes 57614336 | tf_op jit(solution)/shard_map/dot_general | solution.py:327
  333.5 2.9 collective-permute-start.73
  339.0 3.3 collective-permute-done.74
  347.3 4.0 reshape.1016
  351.3 3.4 copy.135
  361.9 2.8 gather_fusion.7
  384.4 3.0 collective-permute-start.88
  396.2 3.0 collective-permute-start.99
  427.6 2.7 collective-permute-start.80
  448.3 3.3 collective-permute-done.96
  464.2 4.9 collective-permute-done.117
  470.4 3.1 collective-permute-done.115
  496.6 18.1 %fusion = f32[7816,768]{1,0:T(8,128)} fusion(bf16[1024,768]{1,0:T(8,128)(2,1)S(1)} %bitcast.765, s32[1024]{0:T(1024)S(1)} %bitcast.759), kind=kOutput, calls=%fused_computation.17 | convolution fusion | flops 12301508608 | bytes 25587712 | tf_op jit(solution)/shard_map/dot_general | solution.py:401
  517.0 2.9 collective-permute-done.122
  (826 shorter events, 304.4 us)
Async XLA Ops:
  31.3 18.5 %collective-permute-start = (bf16[4,128,768]{2,1,0:T(8,128)(2,1)}, bf16[4,128,768]{2,1,0:T(8,128)(2,1)}, u32[]{:S(2)}, u32[]{:S(2)}) collective-permute-start(bf16[4,128,768]{2,1,0:T(8,128)(2,1)} %pad_maximum_fusion.2), channel_id=1, source_target_pairs={{0,4},{4,0},{8,12},{12,8},{16,20},{20,16},{24,28},{28,24},{1,5},{5... | collective-permute-start | bytes 2359304 | tf_op jit(solution)/shard_map/ppermute | solution.py:35
  54.1 7.8 %collective-permute-start.4 = (bf16[2,64,768]{2,1,0:T(8,128)(2,1)S(1)}, bf16[2,64,768]{2,1,0:T(8,128)(2,1)S(1)}, u32[]{:S(2)}, u32[]{:S(2)}) collective-permute-start(bf16[2,64,768]{2,1,0:T(8,128)(2,1)S(1)} %stack.506), channel_id=1, source_target_pairs={{0,16},{4,20},{8,24},{12,28},{16,0},{20,4},{24,8},{28,12},{1,17},{... | collective-permute-start | bytes 589832 | tf_op jit(solution)/shard_map/ppermute | solution.py:35
  54.8 7.9 %collective-permute-start.43 = (bf16[2,64,768]{2,1,0:T(8,128)(2,1)S(1)}, bf16[2,64,768]{2,1,0:T(8,128)(2,1)S(1)}, u32[]{:S(2)}, u32[]{:S(2)}) collective-permute-start(bf16[2,64,768]{2,1,0:T(8,128)(2,1)S(1)} %pad_maximum_fusion.16), channel_id=1, source_target_pairs={{0,8},{4,12},{8,0},{12,4},{16,24},{20,28},{24,16},{28,20},{1,9},{5... | collective-permute-start | bytes 589832 | tf_op jit(solution)/shard_map/ppermute | solution.py:35
  56.3 9.9 %collective-permute-start.46 = (bf16[2,64,768]{2,1,0:T(8,128)(2,1)S(1)}, bf16[2,64,768]{2,1,0:T(8,128)(2,1)S(1)}, u32[]{:S(2)}, u32[]{:S(2)}) collective-permute-start(bf16[2,64,768]{2,1,0:T(8,128)(2,1)S(1)} %stack.508), channel_id=1, source_target_pairs={{0,16},{4,20},{8,24},{12,28},{16,0},{20,4},{24,8},{28,12},{1,17},{... | collective-permute-start | bytes 589832 | tf_op jit(solution)/shard_map/ppermute | solution.py:35
  59.1 9.2 %collective-permute-start.2 = (bf16[1,64,768]{2,1,0:T(8,128)(2,1)S(1)}, bf16[1,64,768]{2,1,0:T(8,128)(2,1)S(1)}, u32[]{:S(2)}, u32[]{:S(2)}) collective-permute-start(bf16[1,64,768]{2,1,0:T(8,128)(2,1)S(1)} %slice.1062), channel_id=1, source_target_pairs={{0,16},{4,20},{8,24},{12,28},{16,0},{20,4},{24,8},{28,12},{1,17},{... | collective-permute-start | bytes 294920 | tf_op jit(solution)/shard_map/ppermute | solution.py:35
  62.0 7.9 %collective-permute-start.5 = (bf16[1,64,768]{2,1,0:T(8,128)(2,1)S(1)}, bf16[1,64,768]{2,1,0:T(8,128)(2,1)S(1)}, u32[]{:S(2)}, u32[]{:S(2)}) collective-permute-start(bf16[1,64,768]{2,1,0:T(8,128)(2,1)S(1)} %slice.1066), channel_id=1, source_target_pairs={{0,8},{4,12},{8,0},{12,4},{16,24},{20,28},{24,16},{28,20},{1,9},{5... | collective-permute-start | bytes 294920 | tf_op jit(solution)/shard_map/ppermute | solution.py:35
  62.7 10.2 %collective-permute-start.44 = (bf16[1,64,768]{2,1,0:T(8,128)(2,1)S(1)}, bf16[1,64,768]{2,1,0:T(8,128)(2,1)S(1)}, u32[]{:S(2)}, u32[]{:S(2)}) collective-permute-start(bf16[1,64,768]{2,1,0:T(8,128)(2,1)S(1)} %slice.1109), channel_id=1, source_target_pairs={{0,16},{4,20},{8,24},{12,28},{16,0},{20,4},{24,8},{28,12},{1,17},{... | collective-permute-start | bytes 294920 | tf_op jit(solution)/shard_map/ppermute | solution.py:35
  66.2 45.5 %collective-permute-start.47 = (bf16[1,64,768]{2,1,0:T(8,128)(2,1)S(1)}, bf16[1,64,768]{2,1,0:T(8,128)(2,1)S(1)}, u32[]{:S(2)}, u32[]{:S(2)}) collective-permute-start(bf16[1,64,768]{2,1,0:T(8,128)(2,1)S(1)} %slice.1113), channel_id=1, source_target_pairs={{0,8},{4,12},{8,0},{12,4},{16,24},{20,28},{24,16},{28,20},{1,9},{5... | collective-permute-start | bytes 294920 | tf_op jit(solution)/shard_map/ppermute | solution.py:35
  92.0 43.1 %collective-permute-start.45 = (bf16[32,768]{1,0:T(8,128)(2,1)S(1)}, bf16[32,768]{1,0:T(8,128)(2,1)S(1)}, u32[]{:S(2)}, u32[]{:S(2)}) collective-permute-start(bf16[32,768]{1,0:T(8,128)(2,1)S(1)} %slice_bitcast_fusion.42), channel_id=1, source_target_pairs={{0,1},{1,0},{2,3},{3,2},{4,5},{5,4},{6,7},{7,6},{8,9},{9,8},{10,11... | collective-permute-start | bytes 147464 | tf_op jit(solution)/shard_map/ppermute | solution.py:35
  226.0 35.5 %collective-permute-start.58 = (bf16[4,128,768]{2,1,0:T(8,128)(2,1)}, bf16[4,128,768]{2,1,0:T(8,128)(2,1)}, u32[]{:S(2)}, u32[]{:S(2)}) collective-permute-start(bf16[4,128,768]{2,1,0:T(8,128)(2,1)} %pad_maximum_fusion.5), channel_id=1, source_target_pairs={{0,4},{4,0},{8,12},{12,8},{16,20},{20,16},{24,28},{28,24},{1,5},{5... | collective-permute-start | bytes 2359304 | tf_op jit(solution)/shard_map/ppermute | solution.py:35
  229.8 8.9 %collective-permute-start.36 = (f32[1,64]{1,0:T(1,128)S(1)}, f32[1,64]{1,0:T(1,128)S(1)}, u32[]{:S(2)}, u32[]{:S(2)}) collective-permute-start(f32[1,64]{1,0:T(1,128)S(1)} %slice.885), channel_id=1, source_target_pairs={{0,16},{4,20},{8,24},{12,28},{16,0},{20,4},{24,8},{28,12},{1,17},{... | collective-permute-start | bytes 776 | tf_op jit(solution)/shard_map/ppermute | solution.py:35
  284.9 33.9 %collective-permute-start.66 = (bf16[32,768]{1,0:T(8,128)(2,1)S(1)}, bf16[32,768]{1,0:T(8,128)(2,1)S(1)}, u32[]{:S(2)}, u32[]{:S(2)}) collective-permute-start(bf16[32,768]{1,0:T(8,128)(2,1)S(1)} %fusion.127), channel_id=1, source_target_pairs={{0,1},{1,0},{2,3},{3,2},{4,5},{5,4},{6,7},{7,6},{8,9},{9,8},{10,11... | collective-permute-start | bytes 147464 | tf_op jit(solution)/shard_map/ppermute | solution.py:35
  285.0 33.8 %collective-permute-start.67 = (bf16[32,768]{1,0:T(8,128)(2,1)S(1)}, bf16[32,768]{1,0:T(8,128)(2,1)S(1)}, u32[]{:S(2)}, u32[]{:S(2)}) collective-permute-start(bf16[32,768]{1,0:T(8,128)(2,1)S(1)} %fusion.127), channel_id=1, source_target_pairs={{0,2},{1,3},{2,0},{3,1},{4,6},{5,7},{6,4},{7,5},{8,10},{9,11},{10,... | collective-permute-start | bytes 147464 | tf_op jit(solution)/shard_map/ppermute | solution.py:35
  287.0 31.8 %collective-permute-start.68 = (bf16[32,768]{1,0:T(8,128)(2,1)S(1)}, bf16[32,768]{1,0:T(8,128)(2,1)S(1)}, u32[]{:S(2)}, u32[]{:S(2)}) collective-permute-start(bf16[32,768]{1,0:T(8,128)(2,1)S(1)} %fusion.127), channel_id=1, source_target_pairs={{0,3},{1,2},{2,1},{3,0},{4,7},{5,6},{6,5},{7,4},{8,11},{9,10},{10,... | collective-permute-start | bytes 147464 | tf_op jit(solution)/shard_map/ppermute | solution.py:35
  357.5 10.3 %collective-permute-start.81 = (bf16[32,768]{1,0:T(8,128)(2,1)}, bf16[32,768]{1,0:T(8,128)(2,1)}, u32[]{:S(2)}, u32[]{:S(2)}) collective-permute-start(bf16[32,768]{1,0:T(8,128)(2,1)} %get-tuple-element.111), channel_id=1, source_target_pairs={{0,1},{1,0},{2,3},{3,2},{4,5},{5,4},{6,7},{7,6},{8,9},{9,8},{10,11... | collective-permute-start | bytes 147464 | tf_op jit(solution)/shard_map/ppermute | solution.py:35
  357.5 10.3 %collective-permute-start.82 = (bf16[32,768]{1,0:T(8,128)(2,1)}, bf16[32,768]{1,0:T(8,128)(2,1)}, u32[]{:S(2)}, u32[]{:S(2)}) collective-permute-start(bf16[32,768]{1,0:T(8,128)(2,1)} %get-tuple-element.113), channel_id=1, source_target_pairs={{0,2},{1,3},{2,0},{3,1},{4,6},{5,7},{6,4},{7,5},{8,10},{9,11},{10,... | collective-permute-start | bytes 147464 | tf_op jit(solution)/shard_map/ppermute | solution.py:35
  359.5 8.3 %collective-permute-start.83 = (bf16[32,768]{1,0:T(8,128)(2,1)}, bf16[32,768]{1,0:T(8,128)(2,1)}, u32[]{:S(2)}, u32[]{:S(2)}) collective-permute-start(bf16[32,768]{1,0:T(8,128)(2,1)} %get-tuple-element.112), channel_id=1, source_target_pairs={{0,3},{1,2},{2,1},{3,0},{4,7},{5,6},{6,5},{7,4},{8,11},{9,10},{10,... | collective-permute-start | bytes 147464 | tf_op jit(solution)/shard_map/ppermute | solution.py:35
  375.5 20.7 %collective-permute-start.75 = (bf16[64,768]{1,0:T(8,128)(2,1)}, bf16[64,768]{1,0:T(8,128)(2,1)}, u32[]{:S(2)}, u32[]{:S(2)}) collective-permute-start(bf16[64,768]{1,0:T(8,128)(2,1)} %get-tuple-element.101), channel_id=1, source_target_pairs={{0,1},{1,0},{2,3},{3,2},{4,5},{5,4},{6,7},{7,6},{8,9},{9,8},{10,11... | collective-permute-start | bytes 294920 | tf_op jit(solution)/shard_map/ppermute | solution.py:35
  375.5 23.7 %collective-permute-start.76 = (bf16[64,768]{1,0:T(8,128)(2,1)}, bf16[64,768]{1,0:T(8,128)(2,1)}, u32[]{:S(2)}, u32[]{:S(2)}) collective-permute-start(bf16[64,768]{1,0:T(8,128)(2,1)} %get-tuple-element.103), channel_id=1, source_target_pairs={{0,2},{1,3},{2,0},{3,1},{4,6},{5,7},{6,4},{7,5},{8,10},{9,11},{10,... | collective-permute-start | bytes 294920 | tf_op jit(solution)/shard_map/ppermute | solution.py:35
  384.4 9.6 %collective-permute-start.88 = (bf16[32,768]{1,0:T(8,128)(2,1)S(1)}, bf16[32,768]{1,0:T(8,128)(2,1)S(1)}, u32[]{:S(2)}, u32[]{:S(2)}) collective-permute-start(bf16[32,768]{1,0:T(8,128)(2,1)S(1)} %get-tuple-element.110), channel_id=1, source_target_pairs={{0,2},{1,3},{2,0},{3,1},{4,6},{5,7},{6,4},{7,5},{8,10},{9,11},{10,... | collective-permute-start | bytes 147464 | tf_op jit(solution)/shard_map/ppermute | solution.py:35
  414.1 72.8 %collective-permute-start.118 = (bf16[4,96,1536]{2,1,0:T(8,128)(2,1)}, bf16[4,96,1536]{2,1,0:T(8,128)(2,1)}, u32[]{:S(2)}, u32[]{:S(2)}) collective-permute-start(bf16[4,96,1536]{2,1,0:T(8,128)(2,1)} %fusion.20), channel_id=1, source_target_pairs={{0,4},{4,0},{8,12},{12,8},{16,20},{20,16},{24,28},{28,24},{1,5},{5... | collective-permute-start | bytes 3538952 | tf_op jit(solution)/shard_map/ppermute | solution.py:35
  414.5 39.8 %collective-permute-start.113 = (bf16[4,96,768]{2,1,0:T(8,128)(2,1)}, bf16[4,96,768]{2,1,0:T(8,128)(2,1)}, u32[]{:S(2)}, u32[]{:S(2)}) collective-permute-start(bf16[4,96,768]{2,1,0:T(8,128)(2,1)} %dynamic-slice_bitcast_fusion), channel_id=1, source_target_pairs={{0,4},{4,0},{8,12},{12,8},{16,20},{20,16},{24,28},{28,24},{1,5},{5... | collective-permute-start | bytes 1769480 | tf_op jit(solution)/shard_map/ppermute | solution.py:35
  414.6 19.6 %collective-permute-start.78 = (bf16[64,768]{1,0:T(8,128)(2,1)S(1)}, bf16[64,768]{1,0:T(8,128)(2,1)S(1)}, u32[]{:S(2)}, u32[]{:S(2)}) collective-permute-start(bf16[64,768]{1,0:T(8,128)(2,1)S(1)} %fusion.57), channel_id=1, source_target_pairs={{0,1},{1,0},{2,3},{3,2},{4,5},{5,4},{6,7},{7,6},{8,9},{9,8},{10,11... | collective-permute-start | bytes 294920 | tf_op jit(solution)/shard_map/ppermute | solution.py:35
  424.6 9.8 %collective-permute-start.79 = (bf16[64,768]{1,0:T(8,128)(2,1)S(1)}, bf16[64,768]{1,0:T(8,128)(2,1)S(1)}, u32[]{:S(2)}, u32[]{:S(2)}) collective-permute-start(bf16[64,768]{1,0:T(8,128)(2,1)S(1)} %fusion.57), channel_id=1, source_target_pairs={{0,2},{1,3},{2,0},{3,1},{4,6},{5,7},{6,4},{7,5},{8,10},{9,11},{10,... | collective-permute-start | bytes 294920 | tf_op jit(solution)/shard_map/ppermute | solution.py:35
  427.6 8.3 %collective-permute-start.80 = (bf16[64,768]{1,0:T(8,128)(2,1)S(1)}, bf16[64,768]{1,0:T(8,128)(2,1)S(1)}, u32[]{:S(2)}, u32[]{:S(2)}) collective-permute-start(bf16[64,768]{1,0:T(8,128)(2,1)S(1)} %fusion.57), channel_id=1, source_target_pairs={{0,3},{1,2},{2,1},{3,0},{4,7},{5,6},{6,5},{7,4},{8,11},{9,10},{10,... | collective-permute-start | bytes 294920 | tf_op jit(solution)/shard_map/ppermute | solution.py:35
  434.3 23.6 %collective-permute-start.108 = (bf16[4,96,768]{2,1,0:T(8,128)(2,1)}, bf16[4,96,768]{2,1,0:T(8,128)(2,1)}, u32[]{:S(2)}, u32[]{:S(2)}) collective-permute-start(bf16[4,96,768]{2,1,0:T(8,128)(2,1)} %dynamic-slice_bitcast_fusion.1), channel_id=1, source_target_pairs={{0,4},{4,0},{8,12},{12,8},{16,20},{20,16},{24,28},{28,24},{1,5},{5... | collective-permute-start | bytes 1769480 | tf_op jit(solution)/shard_map/ppermute | solution.py:35
  436.0 8.4 %collective-permute-start.93 = (bf16[1,64,768]{2,1,0:T(8,128)(2,1)}, bf16[1,64,768]{2,1,0:T(8,128)(2,1)}, u32[]{:S(2)}, u32[]{:S(2)}) collective-permute-start(bf16[1,64,768]{2,1,0:T(8,128)(2,1)} %bitcast.186), channel_id=1, source_target_pairs={{0,8},{4,12},{8,0},{12,4},{16,24},{20,28},{24,16},{28,20},{1,9},{5... | collective-permute-start | bytes 294920 | tf_op jit(solution)/shard_map/ppermute | solution.py:35
  454.3 36.6 %collective-permute-start.97 = (bf16[4,128,768]{2,1,0:T(8,128)(2,1)}, bf16[4,128,768]{2,1,0:T(8,128)(2,1)}, u32[]{:S(2)}, u32[]{:S(2)}) collective-permute-start(bf16[4,128,768]{2,1,0:T(8,128)(2,1)} %pad_maximum_fusion.6), channel_id=1, source_target_pairs={{0,4},{4,0},{8,12},{12,8},{16,20},{20,16},{24,28},{28,24},{1,5},{5... | collective-permute-start | bytes 2359304 | tf_op jit(solution)/shard_map/ppermute | solution.py:35
  460.5 16.9 %collective-permute-start.111 = (bf16[1,2,96,384]{3,2,1,0:T(8,128)(2,1)}, bf16[1,2,96,384]{3,2,1,0:T(8,128)(2,1)}, u32[]{:S(2)}, u32[]{:S(2)}) collective-permute-start(bf16[1,2,96,384]{3,2,1,0:T(8,128)(2,1)} %dynamic-slice_bitcast_fusion.6), channel_id=1, source_target_pairs={{0,16},{4,20},{8,24},{12,28},{16,0},{20,4},{24,8},{28,12},{1,17},{... | collective-permute-start | bytes 442376 | tf_op jit(solution)/shard_map/ppermute | solution.py:35
  461.9 17.9 %collective-permute-start.109 = (bf16[2,1,96,384]{3,2,1,0:T(8,128)(2,1)}, bf16[2,1,96,384]{3,2,1,0:T(8,128)(2,1)}, u32[]{:S(2)}, u32[]{:S(2)}) collective-permute-start(bf16[2,1,96,384]{3,2,1,0:T(8,128)(2,1)} %dynamic-slice_bitcast_fusion.7), channel_id=1, source_target_pairs={{0,8},{4,12},{8,0},{12,4},{16,24},{20,28},{24,16},{28,20},{1,9},{5... | collective-permute-start | bytes 442376 | tf_op jit(solution)/shard_map/ppermute | solution.py:35
  488.7 26.9 %collective-permute-start.119 = (bf16[2,1,96,768]{3,2,1,0:T(8,128)(2,1)S(1)}, bf16[2,1,96,768]{3,2,1,0:T(8,128)(2,1)S(1)}, u32[]{:S(2)}, u32[]{:S(2)}) collective-permute-start(bf16[2,1,96,768]{3,2,1,0:T(8,128)(2,1)S(1)} %dynamic-slice_bitcast_fusion.3), channel_id=1, source_target_pairs={{0,8},{4,12},{8,0},{12,4},{16,24},{20,28},{24,16},{28,20},{1,9},{5... | collective-permute-start | bytes 884744 | tf_op jit(solution)/shard_map/ppermute | solution.py:35
  489.6 25.1 %collective-permute-start.121 = (bf16[1,2,96,768]{3,2,1,0:T(8,128)(2,1)S(1)}, bf16[1,2,96,768]{3,2,1,0:T(8,128)(2,1)S(1)}, u32[]{:S(2)}, u32[]{:S(2)}) collective-permute-start(bf16[1,2,96,768]{3,2,1,0:T(8,128)(2,1)S(1)} %dynamic-slice_bitcast_fusion.2), channel_id=1, source_target_pairs={{0,16},{4,20},{8,24},{12,28},{16,0},{20,4},{24,8},{28,12},{1,17},{... | collective-permute-start | bytes 884744 | tf_op jit(solution)/shard_map/ppermute | solution.py:35
  (229 other events, 2404.7 us)
